TPU v7x, 256 devices: a whole 4x4x8 slice. The times are simulated.
256 devices in a mesh: freq: 64 (over x, z, y_lo), panel: 4 (over y_hi, core).
Axes of the slice: x: 4, y: 4 (y_hi: 2, y_lo: 2; y = y_hi * 2 + y_lo), z: 8, core: 2. Of those that a mesh axis runs over, the one named last changes fastest.
Arguments:
- reflection: bfloat16 [2, 64, 1024, 1024], P(None, 'freq', None, 'panel'), may hold values from -0.1875 to 0.1875
- tile_mask: int32 [64, 16, 16], P('freq', None, 'panel'), may hold values 0 or 1
- focusing: bfloat16 [2, 64, 1024, 256], P(None, 'freq', 'panel'), may hold values from -6 to 6
- initial: float32 [2, 64, 1024, 256], P(None, 'freq', 'panel'), may hold values from -6 to 6
- onsets: int32 [1024, 256], P(('freq', 'panel')), may hold values from 1 to 64
Outputs:
- updated: float32 [2, 64, 1024, 256], P(None, 'freq', 'panel')
All inputs are finite; a program needn't handle non-finite values. No bound on the sum of `tile_mask` on one device may be relied on, other than what follows from the above.
Results may differ from a plain program's by a relative error of at most 0.0015.
Values may be sent and summed in bfloat16 or wider, within the bound.
No kernel may reach another device: no remote copies, remote signals or barrier semaphores. Data moves between devices by JAX's collectives and lax.ppermute only.
A program may use at most 64 MiB of HBM per device.

v0:
```python
import math
import jax
import jax.numpy as jnp
from jax import lax
from jax.sharding import PartitionSpec as P


def tables(length):
    counter = lax.iota(jnp.int32, length)
    product_mod = counter[:, None] * counter[None, :] % length
    angles = product_mod.astype(jnp.float32) * (2.0 * math.pi / length)
    return (jnp.cos(angles), jnp.sin(angles))


def exact_dot(operator_matrix, multiplied_input):
    return jnp.dot(
        operator_matrix,
        multiplied_input,
        precision=lax.Precision.HIGHEST,
        preferred_element_type=jnp.float32,
    )


def window_traces(traces, trace_onsets):
    length = traces.shape[1]
    trace_rows = traces.shape[3] * traces.shape[4]
    flat_rows = traces.reshape(2, length, trace_rows)
    cosine, sine = tables(length)
    real_t = (exact_dot(cosine, flat_rows[0]) - exact_dot(sine, flat_rows[1])) / length
    imaginary_trace_part = (
        exact_dot(sine, flat_rows[0]) + exact_dot(cosine, flat_rows[1])
    ) / length
    window = lax.iota(jnp.int32, length)[:, None] < trace_onsets.reshape(1, trace_rows)
    real_t = jnp.where(window, real_t, 0.0)
    imaginary_trace_part = jnp.where(window, imaginary_trace_part, 0.0)
    out_real = exact_dot(cosine, real_t) + exact_dot(sine, imaginary_trace_part)
    out_imag = exact_dot(cosine, imaginary_trace_part) - exact_dot(sine, real_t)
    return jnp.stack([out_real, out_imag]).astype(jnp.bfloat16).reshape(traces.shape)


def product(operator_matrix, multiplied_input):
    return jnp.einsum(
        "bqx,bxj->bqj", operator_matrix, multiplied_input, preferred_element_type=jnp.float32
    )


def contract(operator_matrix, multiplied_input):
    return jnp.einsum(
        "fabr,fabv->frv", operator_matrix, multiplied_input, preferred_element_type=jnp.float32
    )


def local(reflection, tile_mask, focusing, initial, onsets):
    per_device = reflection.shape[1]
    sources = reflection.shape[2]
    columns = reflection.shape[3]
    tile_edge_length = sources // tile_mask.shape[1]
    points = focusing.shape[3]
    filled = jnp.broadcast_to(
        tile_mask.astype(jnp.bfloat16)[:, :, None, :, None],
        (per_device, tile_mask.shape[1], tile_edge_length, tile_mask.shape[2], tile_edge_length),
    ).reshape(per_device, sources, columns)
    real_r = reflection[0] * filled
    imag_r = reflection[1] * filled
    real_g = product(real_r, focusing[0]) - product(imag_r, focusing[1])
    imag_g = product(real_r, focusing[1]) + product(imag_r, focusing[0])
    groups = lax.axis_size("freq")
    group_rows = sources // groups
    partial_g = jnp.stack([real_g, imag_g]).reshape(2, per_device, groups, group_rows, points)
    summed = lax.psum(partial_g, "panel")
    trace_onsets = lax.all_gather(onsets, "panel", axis=0, tiled=True)
    traces = lax.all_to_all(summed, "freq", split_axis=2, concat_axis=1, tiled=True)
    windowed = window_traces(traces, trace_onsets)
    returned_output = lax.all_to_all(windowed, "freq", split_axis=1, concat_axis=2, tiled=True)
    rows_real = real_r.reshape(per_device, groups, group_rows, columns)
    rows_imag = imag_r.reshape(per_device, groups, group_rows, columns)
    out_real = contract(rows_real, returned_output[0]) + contract(rows_imag, returned_output[1])
    out_imag = contract(rows_real, returned_output[1]) - contract(rows_imag, returned_output[0])
    return initial + jnp.stack([out_real, out_imag])


def solution(mesh):
    return jax.shard_map(
        local,
        mesh=mesh,
        in_specs=(
            P(None, "freq", None, "panel"),
            P("freq", None, "panel"),
            P(None, "freq", "panel", None),
            P(None, "freq", "panel", None),
            P(("freq", "panel"), None),
        ),
        out_specs=P(None, "freq", "panel", None),
        check_vma=False,
    )
```

profile of v0, /device:TPU:2, one launch (start us, length us, event | category | flops | bytes accessed | tf_op | source)
XLA Modules:
  0.0 195.2 jit_solution(1034007891396239297)
XLA Ops:
  6.5 0.8 convert_bitcast_fusion
  7.4 0.3 broadcast_in_dim.19
  7.8 0.7 broadcast_in_dim.20
  9.9 1.5 pad_maximum_fusion
  11.4 66.8 %all-reduce.2.cloned.1.call-done = f32[2,1,64,16,256]{4,3,1,0,2:T(8,128)} async-done(((f32[2,1,64,16,256]{4,3,1,0,2:T(8,128)}), f32[2,1,64,16,256]{4,3,1,0,2:T(8,128)}) %all-reduce.2.cloned.1.call-update) | async-done | bytes 2097168 | tf_op jit(solution)/shard_map/psum | solution.py:70
  78.3 10.6 %all-to-all-start = ((f32[2,1,64,16,256]{4,3,1,0,2:T(8,128)}), f32[2,1,64,16,256]{4,3,1,0,2:T(8,128)S(1)}, u32[]{:S(2)}, u32[]{:S(2)}) async-start(f32[2,1,64,16,256]{4,3,1,0,2:T(8,128)} %all-reduce.2.cloned.1.call-done), calls=%async_computation | async-start | bytes 4194304 | tf_op jit(solution)/shard_map/all_to_all | solution.py:72
  88.9 7.3 %all-gather = s32[4,4,256]{2,1,0:T(4,128)S(1)} all-gather(s32[1,4,256]{2,1,0:T(4,128)S(1)} %bitcast.114), channel_id=1, replica_groups=mesh['freq'=64,'panel'=4] {'panel'}, dimensions={0}, use_global_device_ids=true | all-gather | bytes 20480 | tf_op jit(solution)/shard_map/all_gather | solution.py:71
  96.1 43.7 %all-to-all-done = f32[2,1,64,16,256]{4,3,1,0,2:T(8,128)S(1)} async-done(((f32[2,1,64,16,256]{4,3,1,0,2:T(8,128)}), f32[2,1,64,16,256]{4,3,1,0,2:T(8,128)S(1)}, u32[]{:S(2)}, u32[]{:S(2)}) %all-to-all-start) | async-done | bytes 2097184 | tf_op jit(solution)/shard_map/all_to_all | solution.py:72
  140.0 0.6 copy.35
  140.6 1.2 fusion.41
  141.8 1.2 fusion.37
  142.9 0.6 copy.36
  143.6 1.3 fusion.3
  144.8 1.2 fusion.2
  146.1 1.2 fusion.35
  147.2 1.2 fusion.32
  148.4 1.1 fusion.4
  149.6 1.2 fusion.5
  151.1 34.3 %all_to_all.8 = bf16[2,64,1,16,256]{4,3,2,0,1:T(8,128)(2,1)S(1)} all-to-all(bf16[2,64,1,16,256]{4,3,2,0,1:T(8,128)(2,1)S(1)} %pad_maximum_fusion.1), channel_id=1, replica_groups=mesh['freq'=64,'panel'=4] {'freq'}, dimensions={1} | all-to-all | bytes 2097152 | tf_op jit(solution)/shard_map/all_to_all | solution.py:74
  185.7 0.3 convolution_bitcast_fusion
  186.1 0.3 fusion.9
  186.4 0.3 fusion.7
  186.8 0.7 copy-done.2
  187.5 0.9 maximum_add_fusion
  (21 shorter events, 2.4 us)
Async XLA Ops:
  6.5 1.9 copy-start
  6.5 71.7 %all-reduce.2.cloned.1.call-start = ((), (), s32[]{:S(2)}) async-start(), calls=%async_computation.2 | async-start | bytes 4194304 | tf_op jit(solution)/shard_map/psum | solution.py:70
  7.8 1.0 copy-start.1
  11.4 77.4 %copy-start.3 = (s32[4,256]{1,0:T(4,128)S(1)}, s32[4,256]{1,0:T(4,128)}, u32[]{:S(2)}) copy-start(s32[4,256]{1,0:T(4,128)} %param.9) | copy-start | bytes 12292
  78.3 61.5 %all-to-all-start = ((f32[2,1,64,16,256]{4,3,1,0,2:T(8,128)}), f32[2,1,64,16,256]{4,3,1,0,2:T(8,128)S(1)}, u32[]{:S(2)}, u32[]{:S(2)}) async-start(f32[2,1,64,16,256]{4,3,1,0,2:T(8,128)} %all-reduce.2.cloned.1.call-done), calls=%async_computation | async-start | bytes 4194304 | tf_op jit(solution)/shard_map/all_to_all | solution.py:72
  186.4 1.0 copy-start.2
Sparse Core Ops, SparseCore 0:
  11.5 66.6 all-reduce.1
where the time goes:
time: 195 us
  waiting for transfers between devices  111 us (57%)
  blocking collectives  41.6 us (21%)
  between operations  13.6 us (7%)
  matrix products  12 us (6%)
  starting transfers between devices  10.6 us (5%)
  local copies, waits for them, and re-layouts  3.57 us (2%)
  other arithmetic  3.3 us (2%)
    psum x1, waiting for transfers between devices, local(): summed = lax.psum(partial_g, 'panel')  66.8 us
    all_to_all x1, waiting for transfers between devices, local(): lax.all_to_all(summed, 'freq', split_axis=2, concat_axis=1, tiled=True)  43.7 us
    all_to_all x1, blocking collectives, local(): lax.all_to_all(windowed, 'freq', split_axis=1, concat_axis=2, tiled=True)  34.3 us
    all_to_all x1, starting transfers between devices, local(): lax.all_to_all(summed, 'freq', split_axis=2, concat_axis=1, tiled=True)  10.6 us
    dot_general x8, matrix products, exact_dot(): jnp.dot(operator_matrix, multiplied_input, precision=lax.Precision.HIGHES...  9.47 us
    all_gather x1, blocking collectives, local(): trace_onsets = lax.all_gather(onsets, 'panel', axis=0, tiled=True)  7.27 us
  transfers between devices with their start and end apart: 2, of which 2 were waited for; matrix products, arithmetic and copies ran while one was open for 0% of the time, Pallas kernels for 0%

commit v1 on v0

--- a/solution.py
+++ b/solution.py
@@ -67,7 +67,7 @@
     groups = lax.axis_size("freq")
     group_rows = sources // groups
     partial_g = jnp.stack([real_g, imag_g]).reshape(2, per_device, groups, group_rows, points)
-    summed = lax.psum(partial_g, "panel")
+    summed = jnp.sum(lax.all_gather(partial_g, "panel"), axis=0)
     trace_onsets = lax.all_gather(onsets, "panel", axis=0, tiled=True)
     traces = lax.all_to_all(summed, "freq", split_axis=2, concat_axis=1, tiled=True)
     windowed = window_traces(traces, trace_onsets)

time: 195 us -> 203 us (1.041)
  other arithmetic: 3.3 us -> 8.01 us
    all_gather x0 -> x1, waiting for transfers between devices: none -> 68 us  [local(): summed = jnp.sum(lax.all_gather(partial_g, 'panel'), axis=0)]
    psum x1 -> x0, waiting for transfers between devices: 66.8 us -> none  [local(): summed = lax.psum(partial_g, 'panel')]
    reduce_sum x0 -> x1, other arithmetic: none -> 4.65 us  [local(): summed = jnp.sum(lax.all_gather(partial_g, 'panel'), axis=0)]
where the time goes in v1:
time: 203 us
  waiting for transfers between devices  112 us (55%)
  blocking collectives  41.3 us (20%)
  between operations  13.6 us (7%)
  matrix products  12 us (6%)
  starting transfers between devices  10.7 us (5%)
  other arithmetic  8.01 us (4%)
  local copies, waits for them, and re-layouts  5.17 us (3%)
    all_gather x1, waiting for transfers between devices, local(): summed = jnp.sum(lax.all_gather(partial_g, 'panel'), axis=0)  68 us
    all_to_all x1, waiting for transfers between devices, local(): lax.all_to_all(summed, 'freq', split_axis=2, concat_axis=1, tiled=True)  43.9 us
    all_to_all x1, blocking collectives, local(): lax.all_to_all(windowed, 'freq', split_axis=1, concat_axis=2, tiled=True)  34.2 us
    all_to_all x1, starting transfers between devices, local(): lax.all_to_all(summed, 'freq', split_axis=2, concat_axis=1, tiled=True)  10.7 us
    dot_general x8, matrix products, exact_dot(): jnp.dot(operator_matrix, multiplied_input, precision=lax.Precision.HIGHES...  9.46 us
    all_gather x1, blocking collectives, local(): trace_onsets = lax.all_gather(onsets, 'panel', axis=0, tiled=True)  7.15 us
    reduce_sum x1, other arithmetic, local(): summed = jnp.sum(lax.all_gather(partial_g, 'panel'), axis=0)  4.65 us
  transfers between devices with their start and end apart: 2, of which 2 were waited for; matrix products, arithmetic and copies ran while one was open for 0% of the time, Pallas kernels for 0%

profile of v1, /device:TPU:2, one launch (start us, length us, event | category | flops | bytes accessed | tf_op | source)
XLA Modules:
  0.0 202.7 jit_solution(6182577591667766049)
XLA Ops:
  6.5 0.8 convert_bitcast_fusion
  7.4 0.3 broadcast_in_dim.19
  7.8 0.7 broadcast_in_dim.20
  9.9 1.5 pad_maximum_fusion
  11.5 68.0 %all-gather.3.cloned.1.call-done = f32[4,2,1,64,16,256]{5,4,3,2,1,0:T(8,128)} async-done(((f32[1,2,1,64,16,256]{5,4,3,2,1,0:T(8,128)}), f32[4,2,1,64,16,256]{5,4,3,2,1,0:T(8,128)}) %all-gather.3.cloned.1.call-update) | async-done | bytes 8388624 | tf_op jit(solution)/shard_map/all_gather | solution.py:70
  79.5 4.7 %reduce_sum.11 = f32[2,64,16,256]{3,2,1,0:T(8,128)S(1)} reduce(f32[4,2,1,64,16,256]{5,4,3,2,1,0:T(8,128)} %all-gather.3.cloned.1.call-done, f32[]{:T(128)} %constant.21.clone.1), dimensions={0,2}, to_apply=%region_0.0 | reduce | flops 1572864 | bytes 10485764 | tf_op jit(solution)/shard_map/reduce_sum | solution.py:70
  84.1 1.6 copy.23
  85.7 10.7 %all-to-all-start = ((f32[2,1,64,16,256]{4,3,0,1,2:T(8,128)}), f32[2,1,64,16,256]{4,3,0,1,2:T(8,128)S(1)}, u32[]{:S(2)}, u32[]{:S(2)}) async-start(f32[2,1,64,16,256]{4,3,0,1,2:T(8,128)} %copy.23), calls=%async_computation | async-start | bytes 4194304 | tf_op jit(solution)/shard_map/all_to_all | solution.py:72
  96.4 7.2 %all-gather = s32[4,4,256]{2,1,0:T(4,128)S(1)} all-gather(s32[1,4,256]{2,1,0:T(4,128)S(1)} %bitcast.114), channel_id=1, replica_groups=mesh['freq'=64,'panel'=4] {'panel'}, dimensions={0}, use_global_device_ids=true | all-gather | bytes 20480 | tf_op jit(solution)/shard_map/all_gather | solution.py:71
  103.6 43.9 %all-to-all-done = f32[2,1,64,16,256]{4,3,0,1,2:T(8,128)S(1)} async-done(((f32[2,1,64,16,256]{4,3,0,1,2:T(8,128)}), f32[2,1,64,16,256]{4,3,0,1,2:T(8,128)S(1)}, u32[]{:S(2)}, u32[]{:S(2)}) %all-to-all-start) | async-done | bytes 2097184 | tf_op jit(solution)/shard_map/all_to_all | solution.py:72
  147.6 0.6 copy.31
  148.2 1.2 fusion.37
  149.4 1.1 fusion.41
  150.6 0.6 copy.32
  151.2 1.2 fusion.2
  152.4 1.2 fusion.35
  153.6 1.3 fusion.3
  154.9 1.2 fusion.32
  156.1 1.2 fusion.4
  157.3 1.2 fusion.5
  158.7 34.2 %all_to_all.8 = bf16[2,64,1,16,256]{4,3,2,0,1:T(8,128)(2,1)S(1)} all-to-all(bf16[2,64,1,16,256]{4,3,2,0,1:T(8,128)(2,1)S(1)} %pad_maximum_fusion.1), channel_id=1, replica_groups=mesh['freq'=64,'panel'=4] {'freq'}, dimensions={1} | all-to-all | bytes 2097152 | tf_op jit(solution)/shard_map/all_to_all | solution.py:74
  193.6 0.3 fusion.7
  194.3 0.7 copy-done.2
  195.0 0.9 maximum_add_fusion
  (23 shorter events, 3.1 us)
Async XLA Ops:
  6.5 1.9 copy-start
  6.5 72.9 %all-gather.3.cloned.1.call-start = ((), (), s32[]{:S(2)}) async-start(), calls=%async_computation.2 | async-start | bytes 10485760 | tf_op jit(solution)/shard_map/all_gather | solution.py:70
  7.8 1.0 copy-start.1
  85.7 10.7 %copy-start.3 = (s32[4,256]{1,0:T(4,128)S(1)}, s32[4,256]{1,0:T(4,128)}, u32[]{:S(2)}) copy-start(s32[4,256]{1,0:T(4,128)} %param.9) | copy-start | bytes 12292
  85.7 61.8 %all-to-all-start = ((f32[2,1,64,16,256]{4,3,0,1,2:T(8,128)}), f32[2,1,64,16,256]{4,3,0,1,2:T(8,128)S(1)}, u32[]{:S(2)}, u32[]{:S(2)}) async-start(f32[2,1,64,16,256]{4,3,0,1,2:T(8,128)} %copy.23), calls=%async_computation | async-start | bytes 4194304 | tf_op jit(solution)/shard_map/all_to_all | solution.py:72
  193.9 1.0 copy-start.2
Sparse Core Ops, SparseCore 0:
  11.6 67.8 all-gather.2
